TPU v7x, 128 devices: a whole 4x4x4 slice. The times are simulated.
128 devices in a mesh: slab: 4 (over y_hi, core), orb: 8 (over x, y_lo), pois: 4 (over z).
Axes of the slice: x: 4, y: 4 (y_hi: 2, y_lo: 2; y = y_hi * 2 + y_lo), z: 4, core: 2. Of those that a mesh axis runs over, the one named last changes fastest.
Arguments:
- orbitals: bfloat16 [32, 2, 192, 128, 128], P('orb', None, 'slab', 'pois'), may hold values from -8 to 8
- occupations: float32 [32], P('orb'), may hold values from 5e-05 to 0.0005
- ext_pot: float32 [192, 128, 128], P('slab', 'pois'), may hold values from -1 to 1
- hartree_old: float32 [192, 128, 128], P('slab', 'pois'), may hold values from 0 to 2
Outputs:
- orbitals_new: float32 [32, 2, 192, 128, 128], P('orb', None, 'slab', 'pois')
- hartree_new: float32 [192, 128, 128], P('slab', 'pois', 'orb')
All inputs are finite; a program needn't handle non-finite values.
Results may differ from a plain program's by a relative error of at most 0.0003.
Values may be sent and summed in bfloat16 or wider, within the bound.
No kernel may reach another device: no remote copies, remote signals or barrier semaphores. Data moves between devices by JAX's collectives and lax.ppermute only.
A program may use at most 64 MiB of HBM per device.

v0:
```python
import jax
import jax.numpy as jnp
from jax import lax
from jax.sharding import PartitionSpec as P

NX = 192
NY = 128
NZ = 128
time_step = 0.3


def extended(cells, sides, width):
    for axis, dim in sides:
        count = lax.axis_size(axis)
        ends = count - 1
        head = lax.slice_in_dim(cells, 0, width, axis=dim)
        tail = lax.slice_in_dim(cells, cells.shape[dim] - width, cells.shape[dim], axis=dim)
        cells = jnp.concatenate(
            [
                lax.ppermute(tail, axis, [(i, (i + 1) % count) for i in range(ends)]),
                cells,
                lax.ppermute(head, axis, [((i + 1) % count, i) for i in range(ends)]),
            ],
            axis=dim,
        )
    return cells


def sine_table(row_count, col_start, col_count, length):
    row_index = lax.iota(jnp.int32, row_count) + 1
    col_index = col_start + lax.iota(jnp.int32, col_count) + 1
    product = row_index[:, None] * col_index[None, :] % (2 * (length + 1))
    return jnp.sin(jnp.pi * product.astype(jnp.float32) / (length + 1))


def eigen_values(first_mode, mode_count, length):
    mode_index = first_mode + lax.iota(jnp.int32, mode_count) + 1
    return 2.0 - 2.0 * jnp.cos(jnp.pi * mode_index.astype(jnp.float32) / (length + 1))


def hamiltonian(padded, potential):
    center = padded[:, :, 1:-1, 1:-1, :].astype(jnp.float32)
    z_padded = jnp.pad(center, ((0, 0), (0, 0), (0, 0), (0, 0), (1, 1)))
    beside_all = padded[:, :, 2:, 1:-1, :].astype(jnp.float32) + padded[:, :, :-2, 1:-1, :].astype(
        jnp.float32
    )
    beside_all = (
        beside_all
        + padded[:, :, 1:-1, 2:, :].astype(jnp.float32)
        + padded[:, :, 1:-1, :-2, :].astype(jnp.float32)
    )
    beside_all = beside_all + z_padded[..., 2:] + z_padded[..., :-2]
    return (3.0 + potential) * center - 0.5 * beside_all


def plane_sine(spectrum):
    highest = lax.Precision.HIGHEST
    width_c, width_x, width_y = spectrum.shape
    slab_start = lax.axis_index("slab") * width_x
    pois_start = lax.axis_index("pois") * width_y
    sines_x = sine_table(NX, slab_start, width_x, NX)
    sines_y = sine_table(NY, pois_start, width_y, NY)
    partial_sum = jnp.einsum("ax,cxy->ayc", sines_x, spectrum, precision=highest)
    full_sum = jnp.einsum("by,ayc->abc", sines_y, partial_sum, precision=highest)
    row_blocks = full_sum.reshape(NX // width_x, width_x, NY // width_y, width_y, width_c)
    row_blocks = jnp.transpose(row_blocks, (0, 2, 1, 3, 4)).reshape(-1, width_c)
    result_rows = lax.psum_scatter(row_blocks, ("slab", "pois"), scatter_dimension=0, tiled=True)
    return result_rows.reshape(width_x, width_y, width_c)


def body(orbitals, occupations, ext_pot, hartree_old):
    highest = lax.Precision.HIGHEST
    width_x = orbitals.shape[2]
    width_y = orbitals.shape[3]
    padded = extended(orbitals, (("slab", 2), ("pois", 3)), 1)
    center = padded[:, :, 1:-1, 1:-1, :].astype(jnp.float32)

    def first_image(potential):
        image_one = hamiltonian(padded, potential)
        image_padded = extended(image_one, (("slab", 2), ("pois", 3)), 1)
        return (image_one, image_padded)

    def taylor_step(potential):
        image_one, image_padded = first_image(potential)
        image_two = hamiltonian(image_padded, potential)
        rotated = jnp.stack([image_one[:, 1], -image_one[:, 0]], axis=1)
        return center + time_step * rotated - 0.5 * time_step * time_step * image_two

    pot_start = ext_pot + hartree_old
    predicted = taylor_step(pot_start)
    density_part = jnp.sum(
        occupations[:, None, None, None]
        * (predicted[:, 0] * predicted[:, 0] + predicted[:, 1] * predicted[:, 1]),
        axis=0,
    )
    total = lax.psum(jnp.sum(density_part), ("slab", "orb", "pois"))
    density_part = density_part - total / (NX * NY * NZ) / lax.axis_size("orb")
    full_z = density_part.shape[2]
    width_z = full_z // lax.axis_size("orb")
    sines = sine_table(lax.axis_size("orb") * width_z, 0, full_z, full_z)
    spectrum = lax.psum_scatter(
        jnp.einsum("cz,xyz->cxy", sines, density_part, precision=highest),
        "orb",
        scatter_dimension=0,
        tiled=True,
    )
    spectrum = plane_sine(spectrum)
    slab_start = lax.axis_index("slab") * width_x
    pois_start = lax.axis_index("pois") * width_y
    orb_start = lax.axis_index("orb") * width_z
    divisor = (
        eigen_values(slab_start, width_x, NX)[:, None, None]
        + eigen_values(pois_start, width_y, NY)[None, :, None]
        + eigen_values(orb_start, width_z, NZ)[None, None, :]
    )
    factor = 32.0 * jnp.pi / ((NX + 1) * (NY + 1) * (NZ + 1))
    scaled = jnp.transpose(spectrum * factor / divisor, (2, 0, 1))
    field_part = plane_sine(scaled)
    section = lax.all_gather(field_part, "orb", axis=2, tiled=True)
    sines = sine_table(full_z, jnp.int32(0), section.shape[2], full_z)
    hartree_full = jnp.einsum("zc,xyc->xyz", sines, section, precision=highest)
    pot_middle = ext_pot + 0.5 * (hartree_old + hartree_full)
    orbitals_new = taylor_step(pot_middle)
    hartree_new = lax.dynamic_slice_in_dim(hartree_full, orb_start, width_z, 2)
    return (orbitals_new, hartree_new)


def solution(mesh):
    placed = (
        P("orb", None, "slab", "pois", None),
        P("orb"),
        P("slab", "pois", None),
        P("slab", "pois", None),
    )
    return jax.shard_map(
        body,
        mesh=mesh,
        in_specs=placed,
        out_specs=(P("orb", None, "slab", "pois", None), P("slab", "pois", "orb")),
        check_vma=False,
    )
```

profile of v0, /device:TPU:52, one launch (start us, length us, event | category | flops | bytes accessed | tf_op | source)
XLA Modules:
  0.0 538.2 jit_solution(13242921233021301441)
XLA Ops:
  15.4 5.3 collective-permute-done.1
  31.3 10.8 %multiply_subtract_fusion.1 = (f32[4,2,48,32,128]{4,2,3,1,0:T(8,128)S(1)}, f32[4,2,48,32,128]{4,2,3,1,0:T(8,128)}) fusion(f32[48,32,128]{2,0,1:T(8,128)S(1)} %copy.45, bf16[4,2,48,32,128]{4,3,2,1,0:T(8,128)(2,1)S(1)} %copy-done.2, f32[4,2,48,32,128]{4,2,3,1,0:T(8,128)S(1)} %get-tuple-element.33, bf16[4,2,1,32,128]{4,2,3,1,0:T(2,128)(2,1)S(1)} %collective-permute-done, ...), kind=kLoop, calls=%fused_computation.48 | loop fusion | flops 51904512 | bytes 26288128 | tf_op jit(solution)/shard_map/sub | solution.py:53
  46.7 5.3 collective-permute-done.5
  63.5 9.9 %fusion.8 = f32[4,2,48,32,128]{4,2,3,1,0:T(8,128)S(1)} fusion(f32[4,2,48,32,128]{4,2,3,1,0:T(8,128)S(1)} %get-tuple-element.14, f32[4,2,50,1,128]{4,2,3,1,0:T(8,128)S(1)} %collective-permute-done.7, f32[4,2,1,32,128]{4,2,3,1,0:T(1,128)S(1)} %bitcast.73, f32[4,2,1,32,128]{4,2,3,1,0:T(1,128)S(1)} %bitcast.75, ...), kind=kLoop, calls=%fused_computation.14 | loop fusion | flops 34603008 | bytes 23478272 | tf_op jit(solution)/shard_map/sub | solution.py:87
  75.6 61.9 %psum.7 = f32[]{:T(128)} all-reduce(f32[]{:T(128)} %get-tuple-element.12), channel_id=1, replica_groups=mesh['slab'=4,'orb'=8,'pois'=4] {'slab','orb','pois'}, use_global_device_ids=true, to_apply=%region_2.3 | all-reduce | flops 1 | bytes 8 | tf_op jit(solution)/shard_map/psum | solution.py:96
  139.6 4.7 fusion.26
  144.4 51.7 %reduce-scatter.4.cloned.1.call-done = f32[16,48,32]{1,0,2:T(8,128)} async-done(((f32[128,48,32]{1,0,2:T(8,128)}), f32[16,48,32]{1,0,2:T(8,128)}) %reduce-scatter.4.cloned.1.call-update) | async-done | bytes 98320 | tf_op jit(solution)/shard_map/reduce_scatter | solution.py:101
  201.6 4.1 convolution_bitcast_fusion.1
  208.7 5.4 reshape.112
  214.1 7.1 %copy.62 = f32[4,4,48,32,16]{3,2,1,0,4:T(8,128)} copy(f32[4,4,48,32,16]{2,0,4,3,1:T(4,128)} %bitcast.66) | data formatting | bytes 3145728 | tf_op jit(solution)/shard_map/transpose | solution.py:66
  221.2 5.6 %reshape.113 = f32[24576,16]{0,1:T(8,128)} reshape(f32[4,4,48,32,16]{3,2,1,0,4:T(8,128)} %copy.62) | data formatting | bytes 3145728 | tf_op jit(solution)/shard_map/reshape | solution.py:66
  228.5 66.3 %reduce-scatter.6.cloned.1.call-done = f32[1536,16]{0,1:T(8,128)} async-done(((f32[24576,16]{0,1:T(8,128)}), f32[1536,16]{0,1:T(8,128)}) %reduce-scatter.6.cloned.1.call-update) | async-done | bytes 98320 | tf_op jit(solution)/shard_map/reduce_scatter | solution.py:67
  310.0 5.4 reshape.114
  315.3 7.1 %copy.66 = f32[4,4,48,32,16]{3,2,1,0,4:T(8,128)} copy(f32[4,4,48,32,16]{2,0,4,3,1:T(4,128)} %bitcast.67) | data formatting | bytes 3145728 | tf_op jit(solution)/shard_map/transpose | solution.py:66
  322.4 5.6 %reshape.115 = f32[24576,16]{0,1:T(8,128)} reshape(f32[4,4,48,32,16]{3,2,1,0,4:T(8,128)} %copy.66) | data formatting | bytes 3145728 | tf_op jit(solution)/shard_map/reshape | solution.py:66
  328.1 68.1 %reduce-scatter.8.cloned.1.call-done = f32[1536,16]{0,1:T(8,128)} async-done(((f32[24576,16]{0,1:T(8,128)}), f32[1536,16]{0,1:T(8,128)}) %reduce-scatter.8.cloned.1.call-update) | async-done | bytes 98320 | tf_op jit(solution)/shard_map/reduce_scatter | solution.py:67
  397.4 61.2 %all_gather.3 = f32[48,32,128]{1,2,0:T(8,128)S(1)} all-gather(f32[48,32,16]{1,2,0:T(8,128)S(1)} %copy.67), channel_id=1, replica_groups=mesh['slab'=4,'orb'=8,'pois'=4] {'orb'}, dimensions={2}, use_global_device_ids=true | all-gather | bytes 884736 | tf_op jit(solution)/shard_map/all_gather | solution.py:119
  458.6 7.4 %add_add_fusion = (f32[48,32,128]{2,1,0:T(8,128)S(1)}, f32[48,32,128]{2,1,0:T(8,128)}) fusion(f32[48,32,128]{2,1,0:T(8,128)} %param.6, f32[48,32,128]{2,1,0:T(8,128)} %param.7, f32[48,32,128]{1,2,0:T(8,128)S(1)} %all_gather.3, s32[128]{0:T(128)S(1)} %iota_add_fusion.1), kind=kOutput, calls=%fused_computation.71 | convolution fusion | flops 302923776 | bytes 3932672 | tf_op jit(solution)/shard_map/zc,xyc->xyz/dot_general | solution.py:121
  466.5 4.5 multiply_subtract_fusion
  474.7 4.9 collective-permute-start.8
  482.4 5.0 collective-permute-done.9
  491.2 4.8 collective-permute-start.10
  502.8 24.1 %fusion.14 = f32[4,2,48,32,128]{4,2,3,1,0:T(8,128)S(1)} fusion(f32[4,2,48,32,128]{4,2,3,1,0:T(8,128)} %copy-done, f32[4,2,50,1,128]{4,2,3,1,0:T(8,128)} %collective-permute-done.11, f32[4,2,1,32,128]{4,2,3,1,0:T(1,128)S(1)} %bitcast.69, f32[4,2,1,32,128]{4,2,3,1,0:T(1,128)S(1)} %bitcast.71, f32[4,2,50,1,128]{4,2,3,1,0:T(8,128)} %collective-permute-done.10, ...), kind=kLoop, calls=%fused_computation.20 | loop fusion | flops 34603008 | bytes 23478272 | tf_op jit(solution)/shard_map/sub | solution.py:87
  526.9 4.6 copy.75
  (76 shorter events, 82.4 us)
Async XLA Ops:
  7.2 188.9 %reduce-scatter.4.cloned.1.call-start = ((), (), s32[]{:S(2)}) async-start(), calls=%async_computation.3 | async-start | bytes 2359296 | tf_op jit(solution)/shard_map/reduce_scatter | solution.py:101
  7.2 19.4 %copy-start.5 = (f32[48,32,128]{2,1,0:T(8,128)S(1)}, f32[48,32,128]{2,1,0:T(8,128)}, u32[]{:S(2)}) copy-start(f32[48,32,128]{2,1,0:T(8,128)} %param.6) | copy-start | bytes 2359300
  7.2 19.4 %copy-start.6 = (f32[48,32,128]{2,1,0:T(8,128)S(1)}, f32[48,32,128]{2,1,0:T(8,128)}, u32[]{:S(2)}) copy-start(f32[48,32,128]{2,1,0:T(8,128)} %param.7) | copy-start | bytes 2359300
  10.5 20.7 %copy-start.2 = (bf16[4,2,48,32,128]{4,3,2,1,0:T(8,128)(2,1)S(1)}, bf16[4,2,48,32,128]{4,3,2,1,0:T(8,128)(2,1)}, u32[]{:S(2)}) copy-start(bf16[4,2,48,32,128]{4,3,2,1,0:T(8,128)(2,1)} %param.4) | copy-start | bytes 9437188
  10.8 4.6 collective-permute-start
  12.9 7.8 %collective-permute-start.1 = (bf16[4,2,1,32,128]{4,2,3,1,0:T(2,128)(2,1)S(1)}, bf16[4,2,1,32,128]{4,2,3,1,0:T(2,128)(2,1)S(1)}, u32[]{:S(2)}, u32[]{:S(2)}) collective-permute-start(bf16[4,2,1,32,128]{4,2,3,1,0:T(2,128)(2,1)S(1)} %get-tuple-element.30), channel_id=1, source_target_pairs={{0,32},{32,64},{64,96},{1,33},{33,65},{65,97},{2,34},{34,66},{66,9... | collective-permute-start | bytes 196616 | tf_op jit(solution)/shard_map/ppermute | solution.py:20
  20.7 6.7 %collective-permute-start.3 = (bf16[4,2,50,1,128]{4,2,3,1,0:T(8,128)(2,1)S(1)}, bf16[4,2,50,1,128]{4,2,3,1,0:T(8,128)(2,1)S(1)}, u32[]{:S(2)}, u32[]{:S(2)}) collective-permute-start(bf16[4,2,50,1,128]{4,2,3,1,0:T(8,128)(2,1)S(1)} %get-tuple-element.29), channel_id=1, source_target_pairs={{0,1},{1,2},{2,3},{4,5},{5,6},{6,7},{8,9},{9,10},{10,11},{12,13},{... | collective-permute-start | bytes 307208 | tf_op jit(solution)/shard_map/ppermute | solution.py:20
  24.6 6.7 %collective-permute-start.2 = (bf16[4,2,50,1,128]{4,2,3,1,0:T(8,128)(2,1)S(1)}, bf16[4,2,50,1,128]{4,2,3,1,0:T(8,128)(2,1)S(1)}, u32[]{:S(2)}, u32[]{:S(2)}) collective-permute-start(bf16[4,2,50,1,128]{4,2,3,1,0:T(8,128)(2,1)S(1)} %get-tuple-element.28), channel_id=1, source_target_pairs={{1,0},{2,1},{3,2},{5,4},{6,5},{7,6},{9,8},{10,9},{11,10},{13,12},{... | collective-permute-start | bytes 307208 | tf_op jit(solution)/shard_map/ppermute | solution.py:22
  42.3 4.4 collective-permute-start.4
  44.2 7.8 %collective-permute-start.5 = (f32[4,2,1,32,128]{4,3,2,1,0:T(8,128)S(1)}, f32[4,2,1,32,128]{4,3,2,1,0:T(8,128)S(1)}, u32[]{:S(2)}, u32[]{:S(2)}) collective-permute-start(f32[4,2,1,32,128]{4,3,2,1,0:T(8,128)S(1)} %bitcast.77), channel_id=1, source_target_pairs={{0,32},{32,64},{64,96},{1,33},{33,65},{65,97},{2,34},{34,66},{66,9... | collective-permute-start | bytes 393224 | tf_op jit(solution)/shard_map/ppermute | solution.py:20
  52.1 7.9 %collective-permute-start.7 = (f32[4,2,50,1,128]{4,2,3,1,0:T(8,128)S(1)}, f32[4,2,50,1,128]{4,2,3,1,0:T(8,128)S(1)}, u32[]{:S(2)}, u32[]{:S(2)}) collective-permute-start(f32[4,2,50,1,128]{4,2,3,1,0:T(8,128)S(1)} %get-tuple-element.19), channel_id=1, source_target_pairs={{0,1},{1,2},{2,3},{4,5},{5,6},{6,7},{8,9},{9,10},{10,11},{12,13},{... | collective-permute-start | bytes 614408 | tf_op jit(solution)/shard_map/ppermute | solution.py:20
  55.6 7.9 %collective-permute-start.6 = (f32[4,2,50,1,128]{4,2,3,1,0:T(8,128)S(1)}, f32[4,2,50,1,128]{4,2,3,1,0:T(8,128)S(1)}, u32[]{:S(2)}, u32[]{:S(2)}) collective-permute-start(f32[4,2,50,1,128]{4,2,3,1,0:T(8,128)S(1)} %get-tuple-element.18), channel_id=1, source_target_pairs={{1,0},{2,1},{3,2},{5,4},{6,5},{7,6},{9,8},{10,9},{11,10},{13,12},{... | collective-permute-start | bytes 614408 | tf_op jit(solution)/shard_map/ppermute | solution.py:22
  63.5 10.0 %copy-start.7 = (f32[4]{0:T(128)S(1)}, f32[4]{0:T(128)}, u32[]{:S(2)}) copy-start(f32[4]{0:T(128)} %param.5) | copy-start | bytes 52
  144.3 150.5 %reduce-scatter.6.cloned.1.call-start = ((), (), s32[]{:S(2)}) async-start(), calls=%async_computation.4 | async-start | bytes 1671168 | tf_op jit(solution)/shard_map/reduce_scatter | solution.py:67
  226.8 169.4 %reduce-scatter.8.cloned.1.call-start = ((), (), s32[]{:S(2)}) async-start(), calls=%async_computation.5 | async-start | bytes 1671168 | tf_op jit(solution)/shard_map/reduce_scatter | solution.py:67
  466.5 4.6 copy-start.3
  471.1 2.7 copy-start
  474.7 7.7 %collective-permute-start.8 = (f32[4,2,1,32,128]{4,3,2,1,0:T(8,128)}, f32[4,2,1,32,128]{4,3,2,1,0:T(8,128)S(1)}, u32[]{:S(2)}, u32[]{:S(2)}) collective-permute-start(f32[4,2,1,32,128]{4,3,2,1,0:T(8,128)} %bitcast.17), channel_id=1, source_target_pairs={{32,0},{64,32},{96,64},{33,1},{65,33},{97,65},{34,2},{66,34},{98,6... | collective-permute-start | bytes 393224 | tf_op jit(solution)/shard_map/ppermute | solution.py:22
  479.6 7.8 %collective-permute-start.9 = (f32[4,2,1,32,128]{4,3,2,1,0:T(8,128)S(1)}, f32[4,2,1,32,128]{4,3,2,1,0:T(8,128)S(1)}, u32[]{:S(2)}, u32[]{:S(2)}) collective-permute-start(f32[4,2,1,32,128]{4,3,2,1,0:T(8,128)S(1)} %bitcast.76), channel_id=1, source_target_pairs={{0,32},{32,64},{64,96},{1,33},{33,65},{65,97},{2,34},{34,66},{66,9... | collective-permute-start | bytes 393224 | tf_op jit(solution)/shard_map/ppermute | solution.py:20
  481.5 14.5 %copy-start.1 = (f32[4,2,48,32,128]{4,2,3,1,0:T(8,128)S(1)}, f32[4,2,48,32,128]{4,2,3,1,0:T(8,128)}, u32[]{:S(2)}) copy-start(f32[4,2,48,32,128]{4,2,3,1,0:T(8,128)} %copy-done) | copy-start | bytes 18874372
  489.3 13.5 %collective-permute-start.11 = (f32[4,2,50,1,128]{4,2,3,1,0:T(8,128)}, f32[4,2,50,1,128]{4,2,3,1,0:T(8,128)}, u32[]{:S(2)}, u32[]{:S(2)}) collective-permute-start(f32[4,2,50,1,128]{4,2,3,1,0:T(8,128)} %get-tuple-element.17), channel_id=1, source_target_pairs={{0,1},{1,2},{2,3},{4,5},{5,6},{6,7},{8,9},{9,10},{10,11},{12,13},{... | collective-permute-start | bytes 614408 | tf_op jit(solution)/shard_map/ppermute | solution.py:20
  491.2 8.1 %copy-start.4 = (f32[48,32,128]{2,1,0:T(8,128)S(1)}, f32[48,32,128]{2,1,0:T(8,128)}, u32[]{:S(2)}) copy-start(f32[48,32,128]{2,1,0:T(8,128)} %get-tuple-element.35) | copy-start | bytes 2359300
  491.2 11.5 %collective-permute-start.10 = (f32[4,2,50,1,128]{4,2,3,1,0:T(8,128)}, f32[4,2,50,1,128]{4,2,3,1,0:T(8,128)}, u32[]{:S(2)}, u32[]{:S(2)}) collective-permute-start(f32[4,2,50,1,128]{4,2,3,1,0:T(8,128)} %get-tuple-element.16), channel_id=1, source_target_pairs={{1,0},{2,1},{3,2},{5,4},{6,5},{7,6},{9,8},{10,9},{11,10},{13,12},{... | collective-permute-start | bytes 614408 | tf_op jit(solution)/shard_map/ppermute | solution.py:22
Sparse Core Ops, SparseCore 0:
  144.4 51.6 reduce-scatter.3
  226.9 67.7 reduce-scatter.5
  328.2 67.9 reduce-scatter.7
where the time goes:
time: 546 us; the launch traced here: 538 us
  waiting for transfers between devices  212 us (39%)
  blocking collectives  123 us (23%)
  other arithmetic  65.3 us (12%)
  local copies, waits for them, and re-layouts  63.3 us (12%)
  starting transfers between devices  34.3 us (6%)
  matrix products  25.4 us (5%)
  between operations  15 us (3%)
    reduce_scatter x2, waiting for transfers between devices, plane_sine(): lax.psum_scatter(row_blocks, ('slab', 'pois'), scatter_dimension=0, tiled...  134 us
    psum x1, blocking collectives, body(): total = lax.psum(jnp.sum(density_part), ('slab', 'orb', 'pois'))  61.9 us
    all_gather x1, blocking collectives, body(): section = lax.all_gather(field_part, 'orb', axis=2, tiled=True)  61.2 us
    reduce_scatter x1, waiting for transfers between devices, body(): lax.psum_scatter(jnp.einsum('cz,xyz->cxy', sines, density_part, precision...  51.7 us
    sub x2, other arithmetic, taylor_step(): center + time_step * rotated - 0.5 * time_step * time_step * image_two  34.1 us
    ppermute x6, starting transfers between devices, extended(): lax.ppermute(head, axis, [((i + 1) % count, i) for i in range(ends)])  18 us
    ppermute x6, waiting for transfers between devices, extended(): lax.ppermute(tail, axis, [(i, (i + 1) % count) for i in range(ends)])  17.1 us
    ppermute x6, starting transfers between devices, extended(): lax.ppermute(tail, axis, [(i, (i + 1) % count) for i in range(ends)])  16 us
  transfers between devices with their start and end apart: 15, of which 13 were waited for; matrix products, arithmetic and copies ran while one was open for 2% of the time, Pallas kernels for 0%

commit v1 on v0

--- a/solution.py
+++ b/solution.py
@@ -116,7 +116,9 @@
     factor = 32.0 * jnp.pi / ((NX + 1) * (NY + 1) * (NZ + 1))
     scaled = jnp.transpose(spectrum * factor / divisor, (2, 0, 1))
     field_part = plane_sine(scaled)
-    section = lax.all_gather(field_part, "orb", axis=2, tiled=True)
+    section = jnp.concatenate(
+        lax.all_to_all(jnp.stack([field_part] * lax.axis_size("orb")), "orb", 0, 0), axis=2
+    )
     sines = sine_table(full_z, jnp.int32(0), section.shape[2], full_z)
     hartree_full = jnp.einsum("zc,xyc->xyz", sines, section, precision=highest)
     pot_middle = ext_pot + 0.5 * (hartree_old + hartree_full)

time: 546 us -> 510 us (0.934)
  blocking collectives: 123 us -> 76.9 us
  local copies, waits for them, and re-layouts: 63.3 us -> 75.6 us
    all_gather x1 -> x0, blocking collectives: 61.2 us -> none  [body(): section = lax.all_gather(field_part, 'orb', axis=2, tiled=True)]
    all_to_all x0 -> x1, blocking collectives: none -> 14.9 us  [body(): lax.all_to_all(jnp.stack([field_part] * lax.axis_size('orb')), 'orb', 0, 0)]
    unnamed x18 -> x29, local copies, waits for them, and re-layouts: 9.56 us -> 19.3 us
  transfers between devices with their start and end apart: 15 -> 15, of which waited for: 13 -> 12; matrix products, arithmetic and copies ran while one was open for 2% -> 2% of each run, Pallas kernels for 0% -> 0%
where the time goes in v1:
time: 510 us; the launch traced here: 500 us
  waiting for transfers between devices  211 us (41%)
  blocking collectives  76.9 us (15%)
  local copies, waits for them, and re-layouts  75.6 us (15%)
  other arithmetic  66.7 us (13%)
  starting transfers between devices  32 us (6%)
  matrix products  23.2 us (5%)
  between operations  15 us (3%)
    reduce_scatter x2, waiting for transfers between devices, plane_sine(): lax.psum_scatter(row_blocks, ('slab', 'pois'), scatter_dimension=0, tiled...  134 us
    psum x1, blocking collectives, body(): total = lax.psum(jnp.sum(density_part), ('slab', 'orb', 'pois'))  62 us
    reduce_scatter x1, waiting for transfers between devices, body(): lax.psum_scatter(jnp.einsum('cz,xyz->cxy', sines, density_part, precision...  52 us
    sub x2, other arithmetic, taylor_step(): center + time_step * rotated - 0.5 * time_step * time_step * image_two  32.9 us
    unnamed x29, local copies, waits for them, and re-layouts  19.3 us
    ppermute x6, starting transfers between devices, extended(): lax.ppermute(tail, axis, [(i, (i + 1) % count) for i in range(ends)])  17.7 us
    ppermute x6, waiting for transfers between devices, extended(): lax.ppermute(tail, axis, [(i, (i + 1) % count) for i in range(ends)])  17 us
    all_to_all x1, blocking collectives, body(): lax.all_to_all(jnp.stack([field_part] * lax.axis_size('orb')), 'orb', 0, 0)  14.9 us
  transfers between devices with their start and end apart: 15, of which 12 were waited for; matrix products, arithmetic and copies ran while one was open for 2% of the time, Pallas kernels for 0%

profile of v1, /device:TPU:52, one launch (start us, length us, event | category | flops | bytes accessed | tf_op | source)
XLA Modules:
  0.0 500.2 jit_solution(3905920621618041682)
XLA Ops:
  15.4 5.3 %collective-permute-done.1 = bf16[4,2,1,32,128]{4,2,3,1,0:T(2,128)(2,1)S(1)} collective-permute-done((bf16[4,2,1,32,128]{4,2,3,1,0:T(2,128)(2,1)S(1)}, bf16[4,2,1,32,128]{4,2,3,1,0:T(2,128)(2,1)S(1)}, u32[]{:S(2)}, u32[]{:S(2)}) %collective-permute-start.1) | collective-permute-done | bytes 65568 | tf_op jit(solution)/shard_map/ppermute | solution.py:20
  31.3 10.8 %multiply_subtract_fusion.1 = (f32[4,2,48,32,128]{4,2,3,1,0:T(8,128)S(1)}, f32[4,2,48,32,128]{4,2,3,1,0:T(8,128)}) fusion(f32[48,32,128]{2,0,1:T(8,128)S(1)} %add_add_fusion.1, bf16[4,2,48,32,128]{4,3,2,1,0:T(8,128)(2,1)S(1)} %copy-done.2, f32[4,2,48,32,128]{4,2,3,1,0:T(8,128)S(1)} %get-tuple-element.33, ...), kind=kLoop, calls=%fused_computation.48 | loop fusion | flops 51904512 | bytes 26288128 | tf_op jit(solution)/shard_map/sub | solution.py:53
  46.7 5.3 %collective-permute-done.5 = f32[4,2,1,32,128]{4,3,2,1,0:T(8,128)S(1)} collective-permute-done((f32[4,2,1,32,128]{4,3,2,1,0:T(8,128)S(1)}, f32[4,2,1,32,128]{4,3,2,1,0:T(8,128)S(1)}, u32[]{:S(2)}, u32[]{:S(2)}) %collective-permute-start.5) | collective-permute-done | bytes 131104 | tf_op jit(solution)/shard_map/ppermute | solution.py:20
  63.5 9.9 %fusion.8 = f32[4,2,48,32,128]{4,2,3,1,0:T(8,128)S(1)} fusion(f32[4,2,48,32,128]{4,2,3,1,0:T(8,128)S(1)} %get-tuple-element.14, f32[4,2,50,1,128]{4,2,3,1,0:T(8,128)S(1)} %collective-permute-done.7, f32[4,2,1,32,128]{4,2,3,1,0:T(1,128)S(1)} %bitcast.83, f32[4,2,1,32,128]{4,2,3,1,0:T(1,128)S(1)} %bitcast.85, ...), kind=kLoop, calls=%fused_computation.14 | loop fusion | flops 34603008 | bytes 23478272 | tf_op jit(solution)/shard_map/sub | solution.py:87
  75.6 62.0 %psum.7 = f32[]{:T(128)} all-reduce(f32[]{:T(128)} %get-tuple-element.12), channel_id=1, replica_groups=mesh['slab'=4,'orb'=8,'pois'=4] {'slab','orb','pois'}, use_global_device_ids=true, to_apply=%region_2.3 | all-reduce | flops 1 | bytes 8 | tf_op jit(solution)/shard_map/psum | solution.py:96
  139.7 4.7 fusion.26
  144.4 52.0 %reduce-scatter.4.cloned.1.call-done = f32[16,48,32]{1,0,2:T(8,128)} async-done(((f32[128,48,32]{1,0,2:T(8,128)}), f32[16,48,32]{1,0,2:T(8,128)}) %reduce-scatter.4.cloned.1.call-update) | async-done | bytes 98320 | tf_op jit(solution)/shard_map/reduce_scatter | solution.py:101
  202.0 4.1 convolution_bitcast_fusion.1
  209.1 5.4 %reshape.117 = f32[4,48,4,32,16]{1,0,4,3,2:T(4,128)} reshape(f32[192,128,16]{0,2,1:T(8,128)} %copy.74) | data formatting | bytes 3145728 | tf_op jit(solution)/shard_map/reshape | solution.py:65
  214.5 7.1 %copy.75 = f32[4,4,48,32,16]{3,2,1,0,4:T(8,128)} copy(f32[4,4,48,32,16]{2,0,4,3,1:T(4,128)} %bitcast.75) | data formatting | bytes 3145728 | tf_op jit(solution)/shard_map/transpose | solution.py:66
  221.6 5.6 %reshape.118 = f32[24576,16]{0,1:T(8,128)} reshape(f32[4,4,48,32,16]{3,2,1,0,4:T(8,128)} %copy.75) | data formatting | bytes 3145728 | tf_op jit(solution)/shard_map/reshape | solution.py:66
  228.8 65.8 %reduce-scatter.6.cloned.1.call-done = f32[1536,16]{0,1:T(8,128)} async-done(((f32[24576,16]{0,1:T(8,128)}), f32[1536,16]{0,1:T(8,128)}) %reduce-scatter.6.cloned.1.call-update) | async-done | bytes 98320 | tf_op jit(solution)/shard_map/reduce_scatter | solution.py:67
  302.8 4.1 convolution_bitcast_fusion
  309.9 5.4 %reshape.119 = f32[4,48,4,32,16]{1,0,4,3,2:T(4,128)} reshape(f32[192,128,16]{0,2,1:T(8,128)} %copy.78) | data formatting | bytes 3145728 | tf_op jit(solution)/shard_map/reshape | solution.py:65
  315.3 7.1 %copy.79 = f32[4,4,48,32,16]{3,2,1,0,4:T(8,128)} copy(f32[4,4,48,32,16]{2,0,4,3,1:T(4,128)} %bitcast.76) | data formatting | bytes 3145728 | tf_op jit(solution)/shard_map/transpose | solution.py:66
  322.3 5.6 %reshape.120 = f32[24576,16]{0,1:T(8,128)} reshape(f32[4,4,48,32,16]{3,2,1,0,4:T(8,128)} %copy.79) | data formatting | bytes 3145728 | tf_op jit(solution)/shard_map/reshape | solution.py:66
  328.0 68.1 %reduce-scatter.8.cloned.1.call-done = f32[1536,16]{0,1:T(8,128)} async-done(((f32[24576,16]{0,1:T(8,128)}), f32[1536,16]{0,1:T(8,128)}) %reduce-scatter.8.cloned.1.call-update) | async-done | bytes 98320 | tf_op jit(solution)/shard_map/reduce_scatter | solution.py:67
  400.5 4.0 reshape.126
  404.6 14.9 %all_to_all.5 = f32[8,1,24576]{2,1,0:T(1,128)} all-to-all(f32[8,1,24576]{2,1,0:T(1,128)} %reshape.126), channel_id=1, replica_groups=mesh['slab'=4,'orb'=8,'pois'=4] {'orb'}, dimensions={0} | all-to-all | bytes 1572864 | tf_op jit(solution)/shard_map/all_to_all | solution.py:120
  420.0 4.5 reduce.1
  430.1 5.2 %add_add_fusion = (f32[48,32,128]{2,0,1:T(8,128)S(1)}, f32[48,32,128]{2,0,1:T(8,128)}) fusion(f32[48,32,128]{2,1,0:T(8,128)S(1)} %copy-done.6, f32[48,32,128]{2,1,0:T(8,128)S(1)} %copy-done.8, f32[48,32,128]{0,2,1:T(8,128)S(1)} %bitcast.77, s32[128]{0:T(128)S(1)} %iota_add_fusion.1), kind=kOutput, calls=%fused_computation.71 | convolution fusion | flops 302923776 | bytes 3932672 | tf_op jit(solution)/shard_map/zc,xyc->xyz/dot_general | solution.py:123
  445.5 5.0 collective-permute-done.9
  465.9 22.9 %fusion.14 = f32[4,2,48,32,128]{4,2,3,1,0:T(8,128)S(1)} fusion(f32[4,2,48,32,128]{4,2,3,1,0:T(8,128)} %copy-done, f32[4,2,50,1,128]{4,2,3,1,0:T(8,128)} %collective-permute-done.11, f32[4,2,1,32,128]{4,2,3,1,0:T(1,128)S(1)} %bitcast.79, f32[4,2,1,32,128]{4,2,3,1,0:T(1,128)S(1)} %bitcast.81, f32[4,2,50,1,128]{4,2,3,1,0:T(8,128)} %collective-permute-done.10, ...), kind=kLoop, calls=%fused_computation.20 | loop fusion | flops 34603008 | bytes 23478272 | tf_op jit(solution)/shard_map/sub | solution.py:87
  488.9 4.6 copy.91
  (90 shorter events, 95.7 us)
Async XLA Ops:
  7.2 189.3 %reduce-scatter.4.cloned.1.call-start = ((), (), s32[]{:S(2)}) async-start(), calls=%async_computation.4 | async-start | bytes 2359296 | tf_op jit(solution)/shard_map/reduce_scatter | solution.py:101
  7.2 19.4 %copy-start.5 = (f32[48,32,128]{2,1,0:T(8,128)S(1)}, f32[48,32,128]{2,1,0:T(8,128)}, u32[]{:S(2)}) copy-start(f32[48,32,128]{2,1,0:T(8,128)} %param.6) | copy-start | bytes 2359300
  7.2 19.4 %copy-start.7 = (f32[48,32,128]{2,1,0:T(8,128)S(1)}, f32[48,32,128]{2,1,0:T(8,128)}, u32[]{:S(2)}) copy-start(f32[48,32,128]{2,1,0:T(8,128)} %param.7) | copy-start | bytes 2359300
  10.5 20.7 %copy-start.2 = (bf16[4,2,48,32,128]{4,3,2,1,0:T(8,128)(2,1)S(1)}, bf16[4,2,48,32,128]{4,3,2,1,0:T(8,128)(2,1)}, u32[]{:S(2)}) copy-start(bf16[4,2,48,32,128]{4,3,2,1,0:T(8,128)(2,1)} %param.4) | copy-start | bytes 9437188
  10.8 4.6 collective-permute-start
  12.9 7.8 %collective-permute-start.1 = (bf16[4,2,1,32,128]{4,2,3,1,0:T(2,128)(2,1)S(1)}, bf16[4,2,1,32,128]{4,2,3,1,0:T(2,128)(2,1)S(1)}, u32[]{:S(2)}, u32[]{:S(2)}) collective-permute-start(bf16[4,2,1,32,128]{4,2,3,1,0:T(2,128)(2,1)S(1)} %get-tuple-element.30), channel_id=1, source_target_pairs={{0,32},{32,64},{64,96},{1,33},{33,65},{65,97},{2,34},{34,66},{66,9... | collective-permute-start | bytes 196616 | tf_op jit(solution)/shard_map/ppermute | solution.py:20
  20.7 6.8 %collective-permute-start.3 = (bf16[4,2,50,1,128]{4,2,3,1,0:T(8,128)(2,1)S(1)}, bf16[4,2,50,1,128]{4,2,3,1,0:T(8,128)(2,1)S(1)}, u32[]{:S(2)}, u32[]{:S(2)}) collective-permute-start(bf16[4,2,50,1,128]{4,2,3,1,0:T(8,128)(2,1)S(1)} %get-tuple-element.29), channel_id=1, source_target_pairs={{0,1},{1,2},{2,3},{4,5},{5,6},{6,7},{8,9},{9,10},{10,11},{12,13},{... | collective-permute-start | bytes 307208 | tf_op jit(solution)/shard_map/ppermute | solution.py:20
  24.6 6.7 %collective-permute-start.2 = (bf16[4,2,50,1,128]{4,2,3,1,0:T(8,128)(2,1)S(1)}, bf16[4,2,50,1,128]{4,2,3,1,0:T(8,128)(2,1)S(1)}, u32[]{:S(2)}, u32[]{:S(2)}) collective-permute-start(bf16[4,2,50,1,128]{4,2,3,1,0:T(8,128)(2,1)S(1)} %get-tuple-element.28), channel_id=1, source_target_pairs={{1,0},{2,1},{3,2},{5,4},{6,5},{7,6},{9,8},{10,9},{11,10},{13,12},{... | collective-permute-start | bytes 307208 | tf_op jit(solution)/shard_map/ppermute | solution.py:22
  42.3 4.4 collective-permute-start.4
  44.2 7.8 %collective-permute-start.5 = (f32[4,2,1,32,128]{4,3,2,1,0:T(8,128)S(1)}, f32[4,2,1,32,128]{4,3,2,1,0:T(8,128)S(1)}, u32[]{:S(2)}, u32[]{:S(2)}) collective-permute-start(f32[4,2,1,32,128]{4,3,2,1,0:T(8,128)S(1)} %bitcast.87), channel_id=1, source_target_pairs={{0,32},{32,64},{64,96},{1,33},{33,65},{65,97},{2,34},{34,66},{66,9... | collective-permute-start | bytes 393224 | tf_op jit(solution)/shard_map/ppermute | solution.py:20
  52.1 7.9 %collective-permute-start.7 = (f32[4,2,50,1,128]{4,2,3,1,0:T(8,128)S(1)}, f32[4,2,50,1,128]{4,2,3,1,0:T(8,128)S(1)}, u32[]{:S(2)}, u32[]{:S(2)}) collective-permute-start(f32[4,2,50,1,128]{4,2,3,1,0:T(8,128)S(1)} %get-tuple-element.19), channel_id=1, source_target_pairs={{0,1},{1,2},{2,3},{4,5},{5,6},{6,7},{8,9},{9,10},{10,11},{12,13},{... | collective-permute-start | bytes 614408 | tf_op jit(solution)/shard_map/ppermute | solution.py:20
  55.6 7.9 %collective-permute-start.6 = (f32[4,2,50,1,128]{4,2,3,1,0:T(8,128)S(1)}, f32[4,2,50,1,128]{4,2,3,1,0:T(8,128)S(1)}, u32[]{:S(2)}, u32[]{:S(2)}) collective-permute-start(f32[4,2,50,1,128]{4,2,3,1,0:T(8,128)S(1)} %get-tuple-element.18), channel_id=1, source_target_pairs={{1,0},{2,1},{3,2},{5,4},{6,5},{7,6},{9,8},{10,9},{11,10},{13,12},{... | collective-permute-start | bytes 614408 | tf_op jit(solution)/shard_map/ppermute | solution.py:22
  63.5 10.0 %copy-start.9 = (f32[4]{0:T(128)S(1)}, f32[4]{0:T(128)}, u32[]{:S(2)}) copy-start(f32[4]{0:T(128)} %param.5) | copy-start | bytes 52
  144.4 150.3 %reduce-scatter.6.cloned.1.call-start = ((), (), s32[]{:S(2)}) async-start(), calls=%async_computation.5 | async-start | bytes 1671168 | tf_op jit(solution)/shard_map/reduce_scatter | solution.py:67
  227.2 168.9 %reduce-scatter.8.cloned.1.call-start = ((), (), s32[]{:S(2)}) async-start(), calls=%async_computation.6 | async-start | bytes 1671168 | tf_op jit(solution)/shard_map/reduce_scatter | solution.py:67
  427.9 7.4 %slice-start = ((s8[6291456]{0:T(1024)(128)(4,1)}), s8[4194304]{0:T(1024)(128)(4,1)S(1)}, s32[]{:S(2)}) async-start(s8[6291456]{0:T(1024)(128)(4,1)} %bitcast.73), calls=%async_computation.7 | async-start | bytes 8388608
  429.8 5.5 %slice-start.1 = ((s8[6291456]{0:T(1024)(128)(4,1)}), s8[2097152]{0:T(1024)(128)(4,1)S(1)}, s32[]{:S(2)}) async-start(s8[6291456]{0:T(1024)(128)(4,1)} %bitcast.73), calls=%async_computation.8 | async-start | bytes 4194304
  437.2 2.7 copy-start
  440.8 4.7 collective-permute-start.8
  442.7 7.8 %collective-permute-start.9 = (f32[4,2,1,32,128]{4,3,2,1,0:T(8,128)S(1)}, f32[4,2,1,32,128]{4,3,2,1,0:T(8,128)S(1)}, u32[]{:S(2)}, u32[]{:S(2)}) collective-permute-start(f32[4,2,1,32,128]{4,3,2,1,0:T(8,128)S(1)} %bitcast.86), channel_id=1, source_target_pairs={{0,32},{32,64},{64,96},{1,33},{33,65},{65,97},{2,34},{34,66},{66,9... | collective-permute-start | bytes 393224 | tf_op jit(solution)/shard_map/ppermute | solution.py:20
  445.1 14.2 %copy-start.1 = (f32[4,2,48,32,128]{4,2,3,1,0:T(8,128)S(1)}, f32[4,2,48,32,128]{4,2,3,1,0:T(8,128)}, u32[]{:S(2)}) copy-start(f32[4,2,48,32,128]{4,2,3,1,0:T(8,128)} %copy-done) | copy-start | bytes 18874372
  452.4 13.6 %collective-permute-start.11 = (f32[4,2,50,1,128]{4,2,3,1,0:T(8,128)}, f32[4,2,50,1,128]{4,2,3,1,0:T(8,128)}, u32[]{:S(2)}, u32[]{:S(2)}) collective-permute-start(f32[4,2,50,1,128]{4,2,3,1,0:T(8,128)} %get-tuple-element.17), channel_id=1, source_target_pairs={{0,1},{1,2},{2,3},{4,5},{5,6},{6,7},{8,9},{9,10},{10,11},{12,13},{... | collective-permute-start | bytes 614408 | tf_op jit(solution)/shard_map/ppermute | solution.py:20
  455.5 7.1 %copy-start.4 = (f32[48,32,128]{2,0,1:T(8,128)S(1)}, f32[48,32,128]{2,0,1:T(8,128)}, u32[]{:S(2)}) copy-start(f32[48,32,128]{2,0,1:T(8,128)} %get-tuple-element.35) | copy-start | bytes 2359300
  455.5 10.4 %collective-permute-start.10 = (f32[4,2,50,1,128]{4,2,3,1,0:T(8,128)}, f32[4,2,50,1,128]{4,2,3,1,0:T(8,128)}, u32[]{:S(2)}, u32[]{:S(2)}) collective-permute-start(f32[4,2,50,1,128]{4,2,3,1,0:T(8,128)} %get-tuple-element.16), channel_id=1, source_target_pairs={{1,0},{2,1},{3,2},{5,4},{6,5},{7,6},{9,8},{10,9},{11,10},{13,12},{... | collective-permute-start | bytes 614408 | tf_op jit(solution)/shard_map/ppermute | solution.py:22
  (3 other events, 6.2 us)
Sparse Core Ops, SparseCore 0:
  144.5 51.9 reduce-scatter.3
  227.3 67.2 reduce-scatter.5
  328.1 67.9 reduce-scatter.7
